TPU v7x, 512 devices: a whole 4x8x8 slice. The times are simulated.
512 devices in a mesh: hyp: 8 (over y), prow: 16 (over x, z_lo), pcol: 4 (over z_hi, core).
Axes of the slice: x: 4, y: 8, z: 8 (z_hi: 2, z_lo: 4; z = z_hi * 4 + z_lo), core: 2. Of those that a mesh axis runs over, the one named last changes fastest.
Arguments:
- sigma_rows: bfloat16 [8, 8192, 8192], P('hyp', 'prow', 'pcol'), may hold values from -1 to 1, as said below
- panel: bfloat16 [8, 8192, 2, 384], P('hyp', ('prow', 'pcol')), may hold values from -0.59765625 to 0.59765625
- live_block_rows: int32 [2, 64], P(None, ('prow', 'pcol')), may hold values from 1 to 128, 6144 in all within a row
- inv_diag: bfloat16 [8, 2, 384, 384], P('hyp', None, ('prow', 'pcol')), may hold values from -0.3125 to 0.3125
- quad_weight: float32 [8], P('hyp'), may hold values from 0.05 to 0.5
Outputs:
- sigma_panel: bfloat16 [8, 8192, 2, 384], P('hyp', ('prow', 'pcol'))
- marginal: float32 [2, 384, 384], replicated
Inputs may be any that keep to these rules, and one draw needn't show every extreme that they name: `sigma_rows`: each quadrature point's matrix is symmetric.
All inputs are finite; a program needn't handle non-finite values. No bound on the sum of `live_block_rows` on one device may be relied on, other than what follows from the above.
Results may differ from a plain program's by a relative error of at most 0.0004.
Values may be sent and summed in bfloat16 or wider, within the bound.
A program may use at most 64 MiB of HBM per device.

v0:
```python
import jax
import jax.numpy as jnp
from jax import lax
from jax.sharding import PartitionSpec as P


def cut_along(x, dim, length):
    shape = x.shape
    pieces = x.reshape(*shape[:dim], length, shape[dim] // length, *shape[dim + 1 :])
    return jnp.moveaxis(pieces, dim, 0)


def sent_and_summed(x, axis, dim):
    length = lax.axis_size(axis)
    pieces = lax.all_to_all(cut_along(x, dim, length), axis, 0, 0, tiled=True)
    return jnp.sum(pieces, axis=0)


def on_device(sigma_rows, panel, live_block_rows, inv_diag, quad_weight):
    height = panel.shape[1]
    width = panel.shape[3]
    supernode_list = panel.shape[2]
    offsets = lax.broadcasted_iota(jnp.int32, (height, supernode_list), 0)
    active = offsets < live_block_rows[:, 0][None, :]
    masked_panel = jnp.where(active[:, :, None], panel[0], jnp.zeros_like(panel[0]))
    grid_rows = lax.axis_size("prow")
    column = lax.axis_index("pcol")
    gathered = lax.all_gather(masked_panel, ("prow", "pcol"), axis=0, tiled=True)
    extent = height * grid_rows
    column_panel = lax.dynamic_slice_in_dim(gathered, column * extent, extent, 0)
    flattened = column_panel.reshape(column_panel.shape[0], supernode_list * width)
    covariance_block = sigma_rows[0]
    applied = sent_and_summed(
        jnp.dot(covariance_block, flattened, preferred_element_type=jnp.float32), "pcol", 0
    )
    applied_full = applied.reshape(height, supernode_list, width)
    half_applied_product = applied_full.astype(jnp.bfloat16)
    sigma_panel = jnp.where(
        active[:, :, None], -half_applied_product, jnp.zeros_like(half_applied_product)
    )[None]
    coupling_block = jnp.einsum(
        "vwg,vwe->wge",
        masked_panel.astype(jnp.float32),
        applied_full,
        precision=lax.Precision.HIGHEST,
    )
    inverse_local = inv_diag[0]
    diagonal = jnp.einsum(
        "skp,skq->spq", inverse_local, inverse_local, preferred_element_type=jnp.float32
    )
    partial_sum = coupling_block + diagonal
    marginal = lax.psum(quad_weight[0] * partial_sum, ("hyp", "prow", "pcol"))
    return (sigma_panel, marginal)


def solution(mesh):
    in_specs = (
        P("hyp", "prow", "pcol"),
        P("hyp", ("prow", "pcol"), None, None),
        P(None, ("prow", "pcol")),
        P("hyp", None, ("prow", "pcol"), None),
        P("hyp"),
    )
    out_specs = (P("hyp", ("prow", "pcol"), None, None), P())
    return jax.shard_map(
        on_device, mesh=mesh, in_specs=in_specs, out_specs=out_specs, check_vma=False
    )
```

profile of v0, /device:TPU:1, one launch (start us, length us, event | category | flops | bytes accessed | tf_op | source)
XLA Modules:
  0.0 488.1 jit_solution(7371981305845828398)
XLA Ops:
  7.2 0.0 copy-start
  7.2 0.0 all-gather.2.cloned.1.call-start
  7.2 0.8 iota_compare_fusion
  8.0 1.9 broadcast_select_fusion
  9.9 0.0 all-gather.2.cloned.1.call-update
  10.0 135.1 %all-gather.2.cloned.1.call-done = bf16[8192,2,384]{2,1,0:T(2,128)(2,1)} async-done(((bf16[128,2,384]{2,1,0:T(2,128)(2,1)}), bf16[8192,2,384]{2,1,0:T(2,128)(2,1)}) %all-gather.2.cloned.1.call-update) | async-done | bytes 12582928 | tf_op jit(solution)/shard_map/all_gather | solution.py:28
  145.1 4.7 constant_dynamic-slice_fusion
  149.8 0.6 copy.21
  150.4 0.0 copy-done
  150.4 2.9 fusion
  153.3 0.0 copy-start.2
  153.4 6.0 %all-to-all-start = ((f32[4,128,768]{2,1,0:T(8,128)}), f32[4,128,768]{2,1,0:T(8,128)}, u32[]{:S(2)}, u32[]{:S(2)}) async-start(f32[4,128,768]{2,1,0:T(8,128)} %bitcast.19), calls=%async_computation | async-start | bytes 3145728 | tf_op jit(solution)/shard_map/all_to_all | solution.py:15
  159.4 0.0 all-reduce.2.cloned.1.call-start
  160.0 0.0 copy-done.2
  160.1 0.4 fusion.4
  160.4 0.0 copy-start.1
  160.4 29.1 %all-to-all-done = f32[4,128,768]{2,1,0:T(8,128)} async-done(((f32[4,128,768]{2,1,0:T(8,128)}), f32[4,128,768]{2,1,0:T(8,128)}, u32[]{:S(2)}, u32[]{:S(2)}) %all-to-all-start) | async-done | bytes 1572896 | tf_op jit(solution)/shard_map/all_to_all | solution.py:15
  189.5 2.3 reduce_sum.9
  191.8 1.9 copy.15
  193.7 0.0 copy-done.1
  193.7 2.7 fusion.2
  196.4 0.0 all-reduce.2.cloned.1.call-update
  196.4 1.0 convert_negate_fusion
  197.5 0.1 neg.14
  197.5 1.0 broadcast_select_fusion.1
  198.5 280.4 %all-reduce.2.cloned.1.call-done = f32[2,384,384]{2,1,0:T(8,128)} async-done(((f32[2,384,384]{2,1,0:T(8,128)}), f32[2,384,384]{2,1,0:T(8,128)}) %all-reduce.2.cloned.1.call-update) | async-done | bytes 1179664 | tf_op jit(solution)/shard_map/psum | solution.py:52
  478.9 2.4 copy.28
Async XLA Ops:
  7.2 143.2 %copy-start = (bf16[1,512,2048]{2,1,0:T(8,128)(2,1)S(1)}, bf16[1,512,2048]{2,1,0:T(8,128)(2,1)}, u32[]{:S(2)}) copy-start(bf16[1,512,2048]{2,1,0:T(8,128)(2,1)} %param.5) | copy-start | bytes 6291460
  7.2 137.9 %all-gather.2.cloned.1.call-start = ((), (), s32[]{:S(2)}) async-start(), calls=%async_computation.1 | async-start | bytes 12779520 | tf_op jit(solution)/shard_map/all_gather | solution.py:28
  153.3 6.7 %copy-start.2 = (bf16[1,2,6,384]{3,1,2,0:T(2,128)(2,1)S(1)}, bf16[1,2,6,384]{3,1,2,0:T(2,128)(2,1)}, u32[]{:S(2)}) copy-start(bf16[1,2,6,384]{3,1,2,0:T(2,128)(2,1)} %param.8) | copy-start | bytes 27652
  153.4 36.2 %all-to-all-start = ((f32[4,128,768]{2,1,0:T(8,128)}), f32[4,128,768]{2,1,0:T(8,128)}, u32[]{:S(2)}, u32[]{:S(2)}) async-start(f32[4,128,768]{2,1,0:T(8,128)} %bitcast.19), calls=%async_computation | async-start | bytes 3145728 | tf_op jit(solution)/shard_map/all_to_all | solution.py:15
  159.4 319.5 %all-reduce.2.cloned.1.call-start = ((), (), s32[]{:S(2)}) async-start(), calls=%async_computation.2 | async-start | bytes 2359296 | tf_op jit(solution)/shard_map/psum | solution.py:52
  160.4 33.3 %copy-start.1 = (bf16[128,2,384]{2,1,0:T(2,128)(2,1)S(1)}, bf16[128,2,384]{2,1,0:T(2,128)(2,1)}, u32[]{:S(2)}) copy-start(bf16[128,2,384]{2,1,0:T(2,128)(2,1)} %broadcast_select_fusion) | copy-start | bytes 589828
Sparse Core Ops, SparseCore 0:
  10.7 134.2 all-gather.1
  196.6 282.2 all-reduce.1
where the time goes:
time: 489 us; the launch traced here: 488 us
  waiting for transfers between devices  445 us (91%)
  between operations  14.8 us (3%)
  local copies, waits for them, and re-layouts  9.67 us (2%)
  other arithmetic  6.99 us (1%)
  starting transfers between devices  6.08 us (1%)
  matrix products  6.01 us (1%)
    psum x1, waiting for transfers between devices, on_device(): marginal = lax.psum(quad_weight[0] * partial_sum, ('hyp', 'prow', 'pcol'))  280 us
    all_gather x1, waiting for transfers between devices, on_device(): lax.all_gather(masked_panel, ('prow', 'pcol'), axis=0, tiled=True)  135 us
    all_to_all x1, waiting for transfers between devices, sent_and_summed(): pieces = lax.all_to_all(cut_along(x, dim, length), axis, 0, 0, tiled=True)  29.1 us
  transfers between devices with their start and end apart: 3, of which 3 were waited for; matrix products, arithmetic and copies ran while one was open for 0% of the time, Pallas kernels for 0%

commit v1 on v0

v1 whole, which is shorter than its diff:
```python
import functools

import jax
import jax.numpy as jnp
from jax import lax
from jax.experimental import pallas as pl
from jax.experimental.pallas import tpu as pltpu
from jax.sharding import PartitionSpec as P

MESH = pl.DeviceIdType.MESH
NX, NZ, NY = 4, 8, 8
CHUNKS = 3
T = 128


def place(y, x, z, k):
    return (y, x * 4 + z % 4, (z // 4) * 2 + k)


def remote(src, dst, send, recv, device):
    return pltpu.make_async_remote_copy(
        src_ref=src, dst_ref=dst, send_sem=send, recv_sem=recv, device_id=device, device_id_type=MESH
    )


def arrived(ref, sem):
    pltpu.make_async_copy(ref, ref, sem).wait()


def pairs():
    return [(s, i, j) for s in range(2) for j in range(3) for i in range(j + 1)]


def kernel(
    w, m, inv, sig, out, marg,
    sg, q, f, wp, pr, sb, zb, d, dr, e, xr, e2, zr, yr, g,
    ssig, sloc, s1, r1, s2, r2, s3, r3, s4, r4, s5, r5, s6, r6,
    sa, ra, sx, rx, sz, rz, sy, ry, sgz, rgz, sgx, rgx, sc, rc,
):
    cw = 768 // CHUNKS
    sub = cw // T
    y = lax.axis_index("hyp")
    prow = lax.axis_index("prow")
    pcol = lax.axis_index("pcol")
    x, zl = prow // 4, prow % 4
    zh, k = pcol // 2, pcol % 2
    z = zh * 4 + zl
    slot = zl * 4 + zh * 2
    right, left = (x + 1) % NX, (x + 3) % NX

    barrier = pltpu.get_barrier_semaphore()
    greet = [place(y, x, z, 1 - k)]
    greet += [place(y, (x + a) % NX, z, c) for a in range(1, NX) for c in range(2)]
    greet += [place(y, x, (z + a) % NZ, k) for a in range(1, NZ)]
    greet += [place((y + a) % NY, x, z, k) for a in range(1, NY)]
    for who in greet:
        pl.semaphore_signal(barrier, inc=1, device_id=who, device_id_type=MESH)
    sigma_copy = pltpu.make_async_copy(sig, sg, ssig)
    sigma_copy.start()
    pl.semaphore_wait(barrier, len(greet))

    sends = []

    def go(copy):
        copy.start()
        sends.append(copy)

    kd = x % 2
    half = x // 2
    for ch in range(CHUNKS):
        own = m.at[ch, pl.ds(pl.multiple_of(x * 32, 32), 32)]

        @pl.when(kd == k)
        def _():
            local = pltpu.make_async_copy(own, q.at[ch, half, k], r1.at[ch])
            local.start()

        @pl.when(kd != k)
        def _():
            copy = remote(own, q.at[ch, half, k], s1.at[ch, 0], r1.at[ch], place(y, x, z, 1 - k))
            copy.start()

        for a in range(1, NX):
            xt = (x + a) % NX
            rows = m.at[ch, pl.ds(pl.multiple_of(xt * 32, 32), 32)]
            go(remote(rows, q.at[ch, half, k], s1.at[ch, a], r1.at[ch], place(y, xt, z, kd)))

    weight = w[...]
    for t, (s, i, j) in enumerate(pairs()):
        d[t] = weight * lax.dot_general(
            inv[s, :, i * T:(i + 1) * T], inv[s, :, j * T:(j + 1) * T],
            (((0,), (0,)), ((), ())), preferred_element_type=jnp.float32,
        )

    for ch in range(CHUNKS):
        arrived(q.at[ch], r1.at[ch])
        for n, a in enumerate((4, 3, 5, 2, 6, 1, 7)):
            zt = (z + a) % NZ
            go(remote(
                q.at[ch, zt // 4], f.at[ch, pl.ds(slot, 2), x], s2.at[ch, n], r2.at[ch], place(y, x, zt, k)
            ))
        pltpu.make_async_copy(q.at[ch, zh], f.at[ch, pl.ds(slot, 2), x], r2.at[ch]).start()

    to_right, to_left = place(y, right, z, k), place(y, left, z, k)

    def ring_own(ch):
        arrived(f.at[ch, :, x], r2.at[ch])
        lo, hi = f.at[ch, 0:8, x], f.at[ch, 8:16, x]
        go(remote(lo, lo, s3.at[ch, 0], r3.at[ch, 0], to_right))
        go(remote(hi, hi, s3.at[ch, 1], r3.at[ch, 1], to_left))
        go(remote(hi, hi, s3.at[ch, 2], r3.at[ch, 2], to_right))
        go(remote(lo, lo, s3.at[ch, 3], r3.at[ch, 3], to_left))

    def ring_relay(ch):
        lo, hi = f.at[ch, 0:8, left], f.at[ch, 8:16, right]
        arrived(lo, r3.at[ch, 0])
        go(remote(lo, lo, s4.at[ch, 0], r4.at[ch, 0], to_right))
        arrived(hi, r3.at[ch, 1])
        go(remote(hi, hi, s4.at[ch, 1], r4.at[ch, 1], to_left))

    def multiply(ch):
        far = (x + 2) % NX
        arrived(f.at[ch, 8:16, left], r3.at[ch, 2])
        arrived(f.at[ch, 0:8, right], r3.at[ch, 3])
        arrived(f.at[ch, 0:8, far], r4.at[ch, 0])
        arrived(f.at[ch, 8:16, far], r4.at[ch, 1])
        product = jnp.dot(sg[...], f[ch].reshape(2048, cw), preferred_element_type=jnp.float32)
        wp[ch] = product.reshape(2, 2, T, cw)
        go(remote(wp.at[ch, :, 1 - k], pr.at[ch], s5.at[ch], r5.at[ch], place(y, x, z, 1 - k)))

    def cross(ch):
        arrived(pr.at[ch], r5.at[ch])
        sb[ch] = wp[ch, 1 - zh, k] + pr[ch, 1 - zh]
        go(remote(sb.at[ch], zb.at[ch], s6.at[ch], r6.at[ch], place(y, x, (z + 4) % NZ, k)))

    def finish(ch):
        arrived(zb.at[ch], r6.at[ch])
        applied = (wp[ch, zh, k] + pr[ch, zh]) + zb[ch]
        high = applied.astype(jnp.bfloat16)
        out[ch] = -high
        low = (applied - high.astype(jnp.float32)).astype(jnp.bfloat16)
        for b in range(sub):
            s, j = divmod(ch * sub + b, 3)
            for i in range(j + 1):
                c0, b0 = divmod(s * 3 + i, sub)
                mine = m[c0, :, b0 * T:(b0 + 1) * T]
                dims = (((0,), (0,)), ((), ()))
                tile = lax.dot_general(
                    mine, high[:, b * T:(b + 1) * T], dims, preferred_element_type=jnp.float32
                ) + lax.dot_general(
                    mine, low[:, b * T:(b + 1) * T], dims, preferred_element_type=jnp.float32
                )
                at = pairs().index((s, i, j))
                d[at] = d[at] + weight * tile

    for t in range(CHUNKS + 4):
        if t < CHUNKS:
            ring_own(t)
        if 0 <= t - 1 < CHUNKS:
            ring_relay(t - 1)
        if t == 2:
            sigma_copy.wait()
        if 0 <= t - 2 < CHUNKS:
            multiply(t - 2)
        if 0 <= t - 3 < CHUNKS:
            cross(t - 3)
        if 0 <= t - 4 < CHUNKS:
            finish(t - 4)

    go(remote(d.at[pl.ds((1 - k) * 6, 6)], dr, sa, ra, place(y, x, z, 1 - k)))
    arrived(dr, ra)
    e[...] = (d[pl.ds(k * 6, 6)] + dr[...]).reshape(NX, 192, T)
    for a in range(1, NX):
        xt = (x + a) % NX
        go(remote(e.at[xt], xr.at[a - 1], sx.at[a - 1], rx, place(y, xt, z, k)))
    arrived(xr, rx)
    e2[...] = (((e[x] + xr[0]) + xr[1]) + xr[2]).reshape(NZ, 24, T)
    for a in range(1, NZ):
        zt = (z + a) % NZ
        go(remote(e2.at[zt], zr.at[a - 1], sz.at[a - 1], rz, place(y, x, zt, k)))
    arrived(zr, rz)
    total = e2[z]
    for a in range(NZ - 1):
        total = total + zr[a]
    yr[y] = total
    for a in range(1, NY):
        go(remote(yr.at[y], yr.at[y], sy.at[a - 1], ry, place((y + a) % NY, x, z, k)))
    arrived(yr.at[0:7], ry)
    total = yr[0]
    for a in range(1, NY):
        total = total + yr[a]
    g[k, x, z] = total
    for a in range(1, NZ):
        go(remote(g.at[k, x, z], g.at[k, x, z], sgz.at[a - 1], rgz, place(y, x, (z + a) % NZ, k)))
    arrived(g.at[0, 0, 0:7], rgz)
    for a in range(1, NX):
        go(remote(g.at[k, x], g.at[k, x], sgx.at[a - 1], rgx, place(y, (x + a) % NX, z, k)))
    arrived(g.at[0, 0:3], rgx)
    go(remote(g.at[k], g.at[k], sc, rc, place(y, x, z, 1 - k)))
    arrived(g.at[0], rc)
    for s in range(2):
        whole = g[s].reshape(6, T, T)
        for t, (u, i, j) in enumerate(pairs()[:6]):
            marg[s, i * T:(i + 1) * T, j * T:(j + 1) * T] = whole[t]
            if i != j:
                marg[s, j * T:(j + 1) * T, i * T:(i + 1) * T] = whole[t].T

    for copy in sends:
        copy.wait_send()
    for ch in range(CHUNKS):
        own = m.at[ch, pl.ds(pl.multiple_of(x * 32, 32), 32)]

        @pl.when(kd != k)
        def _():
            remote(own, q.at[ch, half, k], s1.at[ch, 0], r1.at[ch], place(y, x, z, 1 - k)).wait_send()


def on_device(sigma_rows, panel, live_block_rows, inv_diag, quad_weight):
    cw = 768 // CHUNKS
    offsets = lax.broadcasted_iota(jnp.int32, (128, 2, 384), 0)
    active = offsets < live_block_rows[:, 0][None, :, None]
    masked = jnp.where(active, panel[0], jnp.zeros_like(panel[0])).reshape(128, CHUNKS, cw)
    masked = jnp.transpose(masked, (1, 0, 2))
    inv = jnp.pad(inv_diag[0], ((0, 0), (0, 10), (0, 0)))
    weight = jnp.broadcast_to(quad_weight[:, None], (1, 128))
    f32, bf16 = jnp.float32, jnp.bfloat16
    dma = pltpu.SemaphoreType.DMA
    vmem = pl.BlockSpec(memory_space=pltpu.VMEM)
    negated, marginal = pl.pallas_call(
        kernel,
        out_shape=(
            jax.ShapeDtypeStruct((CHUNKS, 128, cw), bf16),
            jax.ShapeDtypeStruct((2, 384, 384), f32),
        ),
        in_specs=[vmem, vmem, vmem, pl.BlockSpec(memory_space=pl.ANY)],
        out_specs=(vmem, vmem),
        scratch_shapes=[
            pltpu.VMEM((512, 2048), bf16),
            pltpu.VMEM((CHUNKS, 2, 2, 32, cw), bf16),
            pltpu.VMEM((CHUNKS, 16, 4, 32, cw), bf16),
            pltpu.VMEM((CHUNKS, 2, 2, T, cw), f32),
            pltpu.VMEM((CHUNKS, 2, T, cw), f32),
            pltpu.VMEM((CHUNKS, T, cw), f32),
            pltpu.VMEM((CHUNKS, T, cw), f32),
            pltpu.VMEM((12, T, T), f32),
            pltpu.VMEM((6, T, T), f32),
            pltpu.VMEM((NX, 192, T), f32),
            pltpu.VMEM((NX - 1, 192, T), f32),
            pltpu.VMEM((NZ, 24, T), f32),
            pltpu.VMEM((NZ - 1, 24, T), f32),
            pltpu.VMEM((NY, 24, T), f32),
            pltpu.VMEM((2, NX, NZ, 24, T), f32),
            dma, dma,
            dma((CHUNKS, 4)), dma((CHUNKS,)),
            dma((CHUNKS, 7)), dma((CHUNKS,)),
            dma((CHUNKS, 4)), dma((CHUNKS, 4)),
            dma((CHUNKS, 2)), dma((CHUNKS, 2)),
            dma((CHUNKS,)), dma((CHUNKS,)),
            dma((CHUNKS,)), dma((CHUNKS,)),
            dma, dma,
            dma((3,)), dma,
            dma((7,)), dma,
            dma((7,)), dma,
            dma((7,)), dma,
            dma((3,)), dma,
            dma, dma,
        ],
        compiler_params=pltpu.CompilerParams(
            collective_id=0, has_side_effects=True, vmem_limit_bytes=56 * 1024 * 1024
        ),
    )(weight, masked, inv, sigma_rows[0])
    applied = jnp.transpose(negated, (1, 0, 2)).reshape(128, 2, 384)
    sigma_panel = jnp.where(active, applied, jnp.zeros_like(applied))[None]
    return (sigma_panel, marginal)


def solution(mesh):
    in_specs = (
        P("hyp", "prow", "pcol"),
        P("hyp", ("prow", "pcol"), None, None),
        P(None, ("prow", "pcol")),
        P("hyp", None, ("prow", "pcol"), None),
        P("hyp"),
    )
    out_specs = (P("hyp", ("prow", "pcol"), None, None), P())
    return jax.shard_map(
        on_device, mesh=mesh, in_specs=in_specs, out_specs=out_specs, check_vma=False
    )
```

time: 489 us -> 118 us (0.24)
  waiting for transfers between devices: 445 us -> 0 us
  Pallas kernels: 0 us -> 109 us
  between operations: 14.8 us -> 1.32 us
  other arithmetic: 6.99 us -> 0.85 us
  starting transfers between devices: 6.08 us -> 0 us
  matrix products: 6.01 us -> 0 us
    psum x1 -> x0, waiting for transfers between devices: 280 us -> none  [on_device(): marginal = lax.psum(quad_weight[0] * partial_sum, ('hyp', 'prow', 'pcol'))]
    all_gather x1 -> x0, waiting for transfers between devices: 135 us -> none  [on_device(): lax.all_gather(masked_panel, ('prow', 'pcol'), axis=0, tiled=True)]
    pallas_call x0 -> x1, Pallas kernels: none -> 109 us  [on_device(): pl.pallas_call(kernel, out_shape=(jax.ShapeDtypeStruct((CHUNKS, 128, cw),...]
    all_to_all x1 -> x0, waiting for transfers between devices: 29.1 us -> none  [sent_and_summed(): pieces = lax.all_to_all(cut_along(x, dim, length), axis, 0, 0, tiled=True)]
    all_to_all x1 -> x0, starting transfers between devices: 6.04 us -> none  [sent_and_summed(): pieces = lax.all_to_all(cut_along(x, dim, length), axis, 0, 0, tiled=True)]
    dot_general x3 -> x0, matrix products: 6.01 us -> none  [the longest x1 2.94 us: on_device(): jnp.dot(covariance_block, flattened, preferred_element_type=jnp.float32)]
  transfers between devices with their start and end apart: 3 -> 0, of which waited for: 3 -> 0; matrix products, arithmetic and copies ran while one was open for 0% -> 0% of each run, Pallas kernels for 0% -> 0%
where the time goes in v1:
time: 118 us
  Pallas kernels  109 us (92%)
  local copies, waits for them, and re-layouts  6.94 us (6%)
  between operations  1.32 us (1%)
    pallas_call x1, Pallas kernels, on_device(): pl.pallas_call(kernel, out_shape=(jax.ShapeDtypeStruct((CHUNKS, 128, cw),...  109 us
    unnamed x8, local copies, waits for them, and re-layouts  3.67 us

profile of v1, /device:TPU:1, one launch (start us, length us, event | category | flops | bytes accessed | tf_op | source)
XLA Modules:
  0.0 118.0 jit_solution(9404770777228403123)
XLA Ops:
  1.3 0.6 broadcast_in_dim.10.w
  1.9 0.7 lt.29
  2.6 0.7 copy.14
  3.3 0.6 pad.4.inv
  3.9 1.1 copy.8
  5.0 0.2 copy.9
  5.2 0.7 fusion.2.m
  5.9 0.0 copy-start.1
  5.9 108.9 %shard_map.68 = (bf16[3,128,256]{2,1,0:T(8,128)(2,1)}, f32[2,384,384]{2,1,0:T(8,128)}) custom-call(f32[1,128]{1,0:T(1,128)} %broadcast_in_dim.10.w, bf16[3,128,256]{2,1,0:T(8,128)(2,1)} %fusion.2.m, bf16[2,16,384]{2,1,0:T(8,128)(2,1)} %pad.4.inv, bf16[512,2048]{1,0:T(8,128)(2,1)} %bitcast.12), custom_call_target="tpu_custom_call" | custom-call | tf_op jit(solution)/shard_map/pallas_call | solution.py:229
  114.8 0.0 copy-start
  114.8 1.2 %copy.11 = bf16[128,3,256]{0,2,1:T(8,128)(2,1)S(1)} copy(bf16[128,3,256]{2,0,1:T(8,128)(2,1)} %bitcast.15) | data formatting | bytes 393216 | tf_op jit(solution)/shard_map/transpose | solution.py:272
  116.0 0.0 copy-done.1
  116.0 0.1 fusion
  116.1 0.8 copy.12
  116.9 0.0 copy-done
  116.9 1.0 copy.17
  (1 shorter events, 0.0 us)
Async XLA Ops:
  5.9 110.1 %copy-start.1 = (s32[2,1]{0,1:T(1,128)S(1)}, s32[2,1]{0,1:T(1,128)}, u32[]{:S(2)}) copy-start(s32[2,1]{0,1:T(1,128)} %param.7) | copy-start | bytes 28
  114.8 2.2 %copy-start = (f32[2,384,384]{2,1,0:T(8,128)S(1)}, f32[2,384,384]{2,1,0:T(8,128)}, u32[]{:S(2)}) copy-start(f32[2,384,384]{2,1,0:T(8,128)} %get-tuple-element.11) | copy-start | bytes 3538948

commit v2 on v0

v2 whole, which is shorter than its diff:
```python
import jax
import jax.numpy as jnp
from jax import lax
from jax.experimental import pallas as pl
from jax.experimental.pallas import tpu as pltpu
from jax.sharding import PartitionSpec as P

MESH = pl.DeviceIdType.MESH
NX, NZ, NY = 4, 8, 8
T = 128
ORDER = (4, 5, 2, 3, 0, 1)
CHUNKS = len(ORDER)
ACROSS = (((0,), (0,)), ((), ()))


def place(y, x, z, k):
    return (y, x * 4 + z % 4, (z // 4) * 2 + k)


def remote(src, dst, send, recv, device):
    return pltpu.make_async_remote_copy(
        src_ref=src, dst_ref=dst, send_sem=send, recv_sem=recv, device_id=device, device_id_type=MESH
    )


def arrived(ref, sem):
    pltpu.make_async_copy(ref, ref, sem).wait()


def split(v):
    high = v.astype(jnp.bfloat16)
    return high, (v - high.astype(jnp.float32)).astype(jnp.bfloat16)


def across(a, parts):
    high, low = parts
    return lax.dot_general(a, high, ACROSS, preferred_element_type=jnp.float32) + lax.dot_general(
        a, low, ACROSS, preferred_element_type=jnp.float32
    )


def kernel(
    w, m, inv, sig, out, marg,
    sg, q, f, wp, pr, sb, zb, ma,
    d0, d1, d2, dr0, dr1, dr2, e0, e1, e2, yr0, yr1, yr2, xs0, xs1, xs2, zs0, zs1, zs2, g0, g1, g2,
    ssig, s1, r1, s2, r2, s3, r3, s4, r4, s5, r5, s6, r6, sm, rm,
    sd, rd, sy, ry, sx, rx, sz, rz, sg2, rg2, sc, rc,
):
    d, dr, e, yr = (d0, d1, d2), (dr0, dr1, dr2), (e0, e1, e2), (yr0, yr1, yr2)
    xs, zs, g = (xs0, xs1, xs2), (zs0, zs1, zs2), (g0, g1, g2)
    y = lax.axis_index("hyp")
    prow = lax.axis_index("prow")
    pcol = lax.axis_index("pcol")
    x, zl = prow // 4, prow % 4
    zh, k = pcol // 2, pcol % 2
    z = zh * 4 + zl
    slot = zl * 4 + zh * 2
    right, left = (x + 1) % NX, (x + 3) % NX
    partner, opposite = place(y, x, z, 1 - k), place(y, x, (z + 4) % NZ, k)

    barrier = pltpu.get_barrier_semaphore()
    greet = [partner]
    greet += [place(y, (x + a) % NX, z, c) for a in range(1, NX) for c in range(2)]
    greet += [place(y, x, (z + a) % NZ, k) for a in range(1, NZ)]
    greet += [place((y + a) % NY, x, z, k) for a in range(1, NY)]
    for who in greet:
        pl.semaphore_signal(barrier, inc=1, device_id=who, device_id_type=MESH)
    sigma_copy = pltpu.make_async_copy(sig, sg, ssig)
    sigma_copy.start()
    pl.semaphore_wait(barrier, len(greet))

    sends = []

    def go(copy):
        copy.start()
        sends.append(copy)

    kd = x % 2
    half = x // 2

    def quarter(c, at):
        return m.at[c, pl.ds(pl.multiple_of(at * 32, 32), 32)]

    for c in ORDER:

        @pl.when(kd == k)
        def _():
            pltpu.make_async_copy(quarter(c, x), q.at[c, half, k], r1.at[c]).start()

        @pl.when(kd != k)
        def _():
            remote(quarter(c, x), q.at[c, half, k], s1.at[c, 0], r1.at[c], partner).start()

        for a in range(1, NX):
            xt = (x + a) % NX
            go(remote(quarter(c, xt), q.at[c, half, k], s1.at[c, a], r1.at[c], place(y, xt, z, kd)))

    weight = w[...]
    for j in range(3):
        for s in range(2):
            for i in range(j + 1):
                d[j][s, i * T:(i + 1) * T] = weight * lax.dot_general(
                    inv[s, :, i * T:(i + 1) * T], inv[s, :, j * T:(j + 1) * T],
                    ACROSS, preferred_element_type=jnp.float32,
                )

    for c in ORDER:
        arrived(q.at[c], r1.at[c])
        for n, a in enumerate((4, 3, 5, 2, 6, 1, 7)):
            zt = (z + a) % NZ
            go(remote(q.at[c, zt // 4], f.at[c, pl.ds(slot, 2), x], s2.at[c, n], r2.at[c], place(y, x, zt, k)))
        pltpu.make_async_copy(q.at[c, zh], f.at[c, pl.ds(slot, 2), x], r2.at[c]).start()
    go(remote(m.at[0:2], ma, sm, rm, opposite))

    to_right, to_left = place(y, right, z, k), place(y, left, z, k)

    def ring_own(c):
        arrived(f.at[c, :, x], r2.at[c])
        lo, hi = f.at[c, 0:8, x], f.at[c, 8:16, x]
        go(remote(lo, lo, s3.at[c, 0], r3.at[c, 0], to_right))
        go(remote(hi, hi, s3.at[c, 1], r3.at[c, 1], to_left))
        go(remote(hi, hi, s3.at[c, 2], r3.at[c, 2], to_right))
        go(remote(lo, lo, s3.at[c, 3], r3.at[c, 3], to_left))

    def ring_relay(c):
        lo, hi = f.at[c, 0:8, left], f.at[c, 8:16, right]
        arrived(lo, r3.at[c, 0])
        go(remote(lo, lo, s4.at[c, 0], r4.at[c, 0], to_right))
        arrived(hi, r3.at[c, 1])
        go(remote(hi, hi, s4.at[c, 1], r4.at[c, 1], to_left))

    def multiply(c):
        far = (x + 2) % NX
        arrived(f.at[c, 8:16, left], r3.at[c, 2])
        arrived(f.at[c, 0:8, right], r3.at[c, 3])
        arrived(f.at[c, 0:8, far], r4.at[c, 0])
        arrived(f.at[c, 8:16, far], r4.at[c, 1])
        product = jnp.dot(sg[...], f[c].reshape(2048, T), preferred_element_type=jnp.float32)
        wp[c] = product.reshape(2, 2, T, T)
        go(remote(wp.at[c, :, 1 - k], pr.at[c], s5.at[c], r5.at[c], partner))

    def cross(c):
        arrived(pr.at[c], r5.at[c])
        theirs = wp[c, 1 - zh, k] + pr[c, 1 - zh]
        sb[c] = theirs
        go(remote(sb.at[c], zb.at[c], s6.at[c], r6.at[c], opposite))
        if c < 2:
            mine = wp[c, zh, k] + pr[c, zh]
            d[0][c] = d[0][c] + weight * (across(m[c], split(mine)) + across(ma[c], split(theirs)))

    def finish(c):
        arrived(zb.at[c], r6.at[c])
        parts = split((wp[c, zh, k] + pr[c, zh]) + zb[c])
        out[c] = -parts[0]
        j, s = divmod(c, 2)
        for i in range(j + 1 if j > 0 else 0):
            rows = pl.ds(i * T, T)
            d[j][s, rows] = d[j][s, rows] + weight * across(m[2 * i + s], parts)

    def sum_core(j):
        go(remote(d[j].at[1 - k], dr[j], sd.at[j], rd.at[j], partner))

    def sum_y(j):
        arrived(dr[j], rd.at[j])
        e[j][...] = (d[j][k] + dr[j][...]).reshape(e[j].shape)
        for n, a in enumerate((4, 3, 5, 2, 6, 1, 7)):
            yt = (y + a) % NY
            go(remote(e[j].at[yt], yr[j].at[n], sy.at[j, n], ry.at[j], place(yt, x, z, k)))

    def sum_x(j):
        arrived(yr[j], ry.at[j])
        total = e[j][y]
        for n in range(NY - 1):
            total = total + yr[j][n]
        xs[j][x] = total
        for n, a in enumerate((2, 1, 3)):
            own = xs[j].at[x]
            go(remote(own, own, sx.at[j, n], rx.at[j], place(y, (x + a) % NX, z, k)))

    def sum_z(j):
        arrived(xs[j].at[0:NX - 1], rx.at[j])
        zs[j][z] = (xs[j][0] + xs[j][1]) + (xs[j][2] + xs[j][3])
        for n, a in enumerate((4, 3, 5, 2, 6, 1, 7)):
            own = zs[j].at[z]
            go(remote(own, own, sz.at[j, n], rz.at[j], place(y, x, (z + a) % NZ, k)))

    def spread_y(j):
        arrived(zs[j].at[0:NZ - 1], rz.at[j])
        total = zs[j][0]
        for n in range(1, NZ):
            total = total + zs[j][n]
        g[j][k, y] = total
        for n, a in enumerate((4, 3, 5, 2, 6, 1, 7)):
            own = g[j].at[k, y]
            go(remote(own, own, sg2.at[j, n], rg2.at[j], place((y + a) % NY, x, z, k)))

    def spread_core(j):
        arrived(g[j].at[0, 0:NY - 1], rg2.at[j])
        go(remote(g[j].at[k], g[j].at[k], sc.at[j], rc.at[j], partner))

    def write(j):
        arrived(g[j].at[0], rc.at[j])
        for s in range(2):
            tiles = g[j][s].reshape(j + 1, T, T)
            for i in range(j + 1):
                marg[s, i * T:(i + 1) * T, j * T:(j + 1) * T] = tiles[i]
                if i != j:
                    marg[s, j * T:(j + 1) * T, i * T:(i + 1) * T] = tiles[i].T

    for t in range(CHUNKS):
        ring_own(ORDER[t])
        if t >= 1:
            ring_relay(ORDER[t - 1])
        if t == 2:
            sigma_copy.wait()
        if t >= 2:
            multiply(ORDER[t - 2])
        if t >= 3:
            cross(ORDER[t - 3])
        if t >= 4:
            finish(ORDER[t - 4])
    sum_core(2)
    ring_relay(ORDER[5])
    multiply(ORDER[4])
    sum_y(2)
    cross(ORDER[3])
    finish(ORDER[2])
    multiply(ORDER[5])
    arrived(ma, rm)
    cross(ORDER[4])
    cross(ORDER[5])
    sum_core(0)
    finish(ORDER[3])
    sum_core(1)
    sum_x(2)
    sum_y(0)
    sum_y(1)
    sum_z(2)
    sum_x(0)
    sum_x(1)
    spread_y(2)
    sum_z(0)
    sum_z(1)
    finish(ORDER[4])
    finish(ORDER[5])
    spread_core(2)
    spread_y(0)
    spread_y(1)
    write(2)
    spread_core(0)
    spread_core(1)
    write(0)
    write(1)

    for copy in sends:
        copy.wait_send()
    for c in ORDER:

        @pl.when(kd != k)
        def _():
            remote(quarter(c, x), q.at[c, half, k], s1.at[c, 0], r1.at[c], partner).wait_send()


def on_device(sigma_rows, panel, live_block_rows, inv_diag, quad_weight):
    offsets = lax.broadcasted_iota(jnp.int32, (128, 2, 384), 0)
    active = offsets < live_block_rows[:, 0][None, :, None]
    masked = jnp.where(active, panel[0], jnp.zeros_like(panel[0])).reshape(128, 2, 3, T)
    masked = jnp.transpose(masked, (2, 1, 0, 3)).reshape(CHUNKS, T, T)
    inv = jnp.pad(inv_diag[0], ((0, 0), (0, 10), (0, 0)))
    weight = jnp.broadcast_to(quad_weight[:, None], (1, 128))
    f32, bf16 = jnp.float32, jnp.bfloat16
    dma = pltpu.SemaphoreType.DMA
    vmem = pl.BlockSpec(memory_space=pltpu.VMEM)
    rows = [(j + 1) * T for j in range(3)]
    negated, marginal = pl.pallas_call(
        kernel,
        out_shape=(
            jax.ShapeDtypeStruct((CHUNKS, T, T), bf16),
            jax.ShapeDtypeStruct((2, 384, 384), f32),
        ),
        in_specs=[vmem, vmem, vmem, pl.BlockSpec(memory_space=pl.ANY)],
        out_specs=(vmem, vmem),
        scratch_shapes=[
            pltpu.VMEM((512, 2048), bf16),
            pltpu.VMEM((CHUNKS, 2, 2, 32, T), bf16),
            pltpu.VMEM((CHUNKS, 16, 4, 32, T), bf16),
            pltpu.VMEM((CHUNKS, 2, 2, T, T), f32),
            pltpu.VMEM((CHUNKS, 2, T, T), f32),
            pltpu.VMEM((CHUNKS, T, T), f32),
            pltpu.VMEM((CHUNKS, T, T), f32),
            pltpu.VMEM((2, T, T), bf16),
        ]
        + [pltpu.VMEM((2, r, T), f32) for r in rows]
        + [pltpu.VMEM((r, T), f32) for r in rows]
        + [pltpu.VMEM((NY, r // NY, T), f32) for r in rows]
        + [pltpu.VMEM((NY - 1, r // NY, T), f32) for r in rows]
        + [pltpu.VMEM((NX, r // NY, T), f32) for r in rows]
        + [pltpu.VMEM((NZ, r // NY, T), f32) for r in rows]
        + [pltpu.VMEM((2, NY, r // NY, T), f32) for r in rows]
        + [
            dma,
            dma((CHUNKS, 4)), dma((CHUNKS,)),
            dma((CHUNKS, 7)), dma((CHUNKS,)),
            dma((CHUNKS, 4)), dma((CHUNKS, 4)),
            dma((CHUNKS, 2)), dma((CHUNKS, 2)),
            dma((CHUNKS,)), dma((CHUNKS,)),
            dma((CHUNKS,)), dma((CHUNKS,)),
            dma, dma,
            dma((3,)), dma((3,)),
            dma((3, 7)), dma((3,)),
            dma((3, 3)), dma((3,)),
            dma((3, 7)), dma((3,)),
            dma((3, 7)), dma((3,)),
            dma((3,)), dma((3,)),
        ],
        compiler_params=pltpu.CompilerParams(
            collective_id=0, has_side_effects=True, vmem_limit_bytes=56 * 1024 * 1024
        ),
    )(weight, masked, inv, sigma_rows[0])
    applied = jnp.transpose(negated.reshape(3, 2, T, T), (2, 1, 0, 3)).reshape(128, 2, 384)
    sigma_panel = jnp.where(active, applied, jnp.zeros_like(applied))[None]
    return (sigma_panel, marginal)


def solution(mesh):
    in_specs = (
        P("hyp", "prow", "pcol"),
        P("hyp", ("prow", "pcol"), None, None),
        P(None, ("prow", "pcol")),
        P("hyp", None, ("prow", "pcol"), None),
        P("hyp"),
    )
    out_specs = (P("hyp", ("prow", "pcol"), None, None), P())
    return jax.shard_map(
        on_device, mesh=mesh, in_specs=in_specs, out_specs=out_specs, check_vma=False
    )
```

time: 489 us -> 97.6 us (0.20)
  waiting for transfers between devices: 445 us -> 0 us
  Pallas kernels: 0 us -> 88.3 us
  between operations: 14.8 us -> 1.31 us
  other arithmetic: 6.99 us -> 0.88 us
  starting transfers between devices: 6.08 us -> 0 us
  matrix products: 6.01 us -> 0 us
    psum x1 -> x0, waiting for transfers between devices: 280 us -> none  [on_device(): marginal = lax.psum(quad_weight[0] * partial_sum, ('hyp', 'prow', 'pcol'))]
    all_gather x1 -> x0, waiting for transfers between devices: 135 us -> none  [on_device(): lax.all_gather(masked_panel, ('prow', 'pcol'), axis=0, tiled=True)]
    pallas_call x0 -> x1, Pallas kernels: none -> 88.3 us  [on_device(): pl.pallas_call(kernel, out_shape=(jax.ShapeDtypeStruct((CHUNKS, T, T), bf...]
    all_to_all x1 -> x0, waiting for transfers between devices: 29.1 us -> none  [sent_and_summed(): pieces = lax.all_to_all(cut_along(x, dim, length), axis, 0, 0, tiled=True)]
    all_to_all x1 -> x0, starting transfers between devices: 6.04 us -> none  [sent_and_summed(): pieces = lax.all_to_all(cut_along(x, dim, length), axis, 0, 0, tiled=True)]
    dot_general x3 -> x0, matrix products: 6.01 us -> none  [the longest x1 2.94 us: on_device(): jnp.dot(covariance_block, flattened, preferred_element_type=jnp.float32)]
  transfers between devices with their start and end apart: 3 -> 0, of which waited for: 3 -> 0; matrix products, arithmetic and copies ran while one was open for 0% -> 0% of each run, Pallas kernels for 0% -> 0%
where the time goes in v2:
time: 97.6 us; the launch traced here: 97.4 us
  Pallas kernels  88.3 us (90%)
  local copies, waits for them, and re-layouts  6.88 us (7%)
  between operations  1.31 us (1%)
    pallas_call x1, Pallas kernels, on_device(): pl.pallas_call(kernel, out_shape=(jax.ShapeDtypeStruct((CHUNKS, T, T), bf...  88.3 us
    unnamed x8, local copies, waits for them, and re-layouts  3.67 us

profile of v2, /device:TPU:1, one launch (start us, length us, event | category | flops | bytes accessed | tf_op | source)
XLA Modules:
  0.0 97.4 jit_solution(7211030688800842935)
XLA Ops:
  1.3 0.6 broadcast_in_dim.10.w
  1.9 0.7 copy.16
  2.6 0.6 pad.4.inv
  3.2 1.1 %copy.10 = bf16[1,128,2,384]{1,3,2,0:T(8,128)(2,1)S(1)} copy(bf16[1,128,2,384]{3,2,1,0:T(2,128)(2,1)} %param.6) | data formatting | bytes 393216 | tf_op args[1]
  4.3 0.8 fusion.2
  5.0 0.8 copy.11
  5.9 0.0 copy-start.1
  5.9 88.3 %shard_map.68 = (bf16[6,128,128]{2,1,0:T(8,128)(2,1)}, f32[2,384,384]{2,1,0:T(8,128)}) custom-call(f32[1,128]{1,0:T(1,128)} %broadcast_in_dim.10.w, bf16[6,128,128]{2,1,0:T(8,128)(2,1)} %bitcast.17, bf16[2,16,384]{2,1,0:T(8,128)(2,1)} %pad.4.inv, bf16[512,2048]{1,0:T(8,128)(2,1)} %bitcast.16), custom_call_target="tpu_custom_call" | custom-call | tf_op jit(solution)/shard_map/pallas_call | solution.py:275
  94.2 0.0 copy-start
  94.2 1.2 %copy.13 = bf16[3,2,128,128]{2,3,0,1:T(8,128)(2,1)S(1)} copy(bf16[3,2,128,128]{3,2,1,0:T(8,128)(2,1)} %bitcast.19) | data formatting | bytes 393216 | tf_op jit(solution)/shard_map/reshape | solution.py:320
  95.4 0.0 copy-done.1
  95.4 0.1 fusion
  95.5 0.8 copy.14
  96.4 0.0 copy-done
  96.4 1.0 %copy.19 = f32[2,384,384]{2,1,0:T(8,128)} copy(f32[2,384,384]{2,1,0:T(8,128)S(1)} %copy-done) | data formatting | bytes 2359296
Async XLA Ops:
  5.9 89.5 %copy-start.1 = (s32[2,1]{0,1:T(1,128)S(1)}, s32[2,1]{0,1:T(1,128)}, u32[]{:S(2)}) copy-start(s32[2,1]{0,1:T(1,128)} %param.7) | copy-start | bytes 28
  94.2 2.2 %copy-start = (f32[2,384,384]{2,1,0:T(8,128)S(1)}, f32[2,384,384]{2,1,0:T(8,128)}, u32[]{:S(2)}) copy-start(f32[2,384,384]{2,1,0:T(8,128)} %get-tuple-element.11) | copy-start | bytes 3538948

commit v3 on v2

--- a/solution.py
+++ b/solution.py
@@ -40,8 +40,8 @@
 
 
 def kernel(
-    w, m, inv, sig, out, marg,
-    sg, q, f, wp, pr, sb, zb, ma,
+    w, live, panel, inv, sig, out, marg,
+    m, iv, ob, sg, q, f, wp, pr, sb, zb, ma,
     d0, d1, d2, dr0, dr1, dr2, e0, e1, e2, yr0, yr1, yr2, xs0, xs1, xs2, zs0, zs1, zs2, g0, g1, g2,
     ssig, s1, r1, s2, r2, s3, r3, s4, r4, s5, r5, s6, r6, sm, rm,
     sd, rd, sy, ry, sx, rx, sz, rz, sg2, rg2, sc, rc,
@@ -67,6 +67,13 @@
         pl.semaphore_signal(barrier, inc=1, device_id=who, device_id_type=MESH)
     sigma_copy = pltpu.make_async_copy(sig, sg, ssig)
     sigma_copy.start()
+    weight = w[0]
+    rows = lax.broadcasted_iota(jnp.int32, (T, T), 0)
+    active = [rows < live[s] for s in range(2)]
+    for j in range(3):
+        both = panel[:, :, j * T:(j + 1) * T].astype(jnp.float32)
+        for s in range(2):
+            m[2 * j + s] = jnp.where(active[s], both[:, s, :], 0.0).astype(jnp.bfloat16)
     pl.semaphore_wait(barrier, len(greet))
 
     sends = []
@@ -95,13 +102,15 @@
             xt = (x + a) % NX
             go(remote(quarter(c, xt), q.at[c, half, k], s1.at[c, a], r1.at[c], place(y, xt, z, kd)))
 
-    weight = w[...]
-    for j in range(3):
-        for s in range(2):
+    iv[...] = jnp.zeros_like(iv)
+    both = inv[...].astype(jnp.float32)
+    for s in range(2):
+        iv[s, 0:6] = both[:, s, :]
+        own = iv[s].astype(jnp.bfloat16)
+        for j in range(3):
             for i in range(j + 1):
                 d[j][s, i * T:(i + 1) * T] = weight * lax.dot_general(
-                    inv[s, :, i * T:(i + 1) * T], inv[s, :, j * T:(j + 1) * T],
-                    ACROSS, preferred_element_type=jnp.float32,
+                    own[:, i * T:(i + 1) * T], own[:, j * T:(j + 1) * T], ACROSS, preferred_element_type=jnp.float32
                 )
 
     for c in ORDER:
@@ -151,8 +160,12 @@
     def finish(c):
         arrived(zb.at[c], r6.at[c])
         parts = split((wp[c, zh, k] + pr[c, zh]) + zb[c])
-        out[c] = -parts[0]
         j, s = divmod(c, 2)
+        negated = jnp.where(active[s], -parts[0].astype(jnp.float32), 0.0)
+        if s == 0:
+            ob[j] = negated
+        else:
+            out[:, :, j * T:(j + 1) * T] = jnp.stack([ob[j], negated], axis=1).astype(jnp.bfloat16)
         for i in range(j + 1 if j > 0 else 0):
             rows = pl.ds(i * T, T)
             d[j][s, rows] = d[j][s, rows] + weight * across(m[2 * i + s], parts)
@@ -262,25 +275,23 @@
 
 
 def on_device(sigma_rows, panel, live_block_rows, inv_diag, quad_weight):
-    offsets = lax.broadcasted_iota(jnp.int32, (128, 2, 384), 0)
-    active = offsets < live_block_rows[:, 0][None, :, None]
-    masked = jnp.where(active, panel[0], jnp.zeros_like(panel[0])).reshape(128, 2, 3, T)
-    masked = jnp.transpose(masked, (2, 1, 0, 3)).reshape(CHUNKS, T, T)
-    inv = jnp.pad(inv_diag[0], ((0, 0), (0, 10), (0, 0)))
-    weight = jnp.broadcast_to(quad_weight[:, None], (1, 128))
     f32, bf16 = jnp.float32, jnp.bfloat16
     dma = pltpu.SemaphoreType.DMA
     vmem = pl.BlockSpec(memory_space=pltpu.VMEM)
+    smem = pl.BlockSpec(memory_space=pltpu.SMEM)
     rows = [(j + 1) * T for j in range(3)]
-    negated, marginal = pl.pallas_call(
+    sigma_panel, marginal = pl.pallas_call(
         kernel,
         out_shape=(
-            jax.ShapeDtypeStruct((CHUNKS, T, T), bf16),
+            jax.ShapeDtypeStruct((T, 2, 384), bf16),
             jax.ShapeDtypeStruct((2, 384, 384), f32),
         ),
-        in_specs=[vmem, vmem, vmem, pl.BlockSpec(memory_space=pl.ANY)],
+        in_specs=[smem, smem, vmem, vmem, pl.BlockSpec(memory_space=pl.ANY)],
         out_specs=(vmem, vmem),
         scratch_shapes=[
+            pltpu.VMEM((CHUNKS, T, T), bf16),
+            pltpu.VMEM((2, 8, 384), f32),
+            pltpu.VMEM((3, T, T), f32),
             pltpu.VMEM((512, 2048), bf16),
             pltpu.VMEM((CHUNKS, 2, 2, 32, T), bf16),
             pltpu.VMEM((CHUNKS, 16, 4, 32, T), bf16),
@@ -316,10 +327,8 @@
         compiler_params=pltpu.CompilerParams(
             collective_id=0, has_side_effects=True, vmem_limit_bytes=56 * 1024 * 1024
         ),
-    )(weight, masked, inv, sigma_rows[0])
-    applied = jnp.transpose(negated.reshape(3, 2, T, T), (2, 1, 0, 3)).reshape(128, 2, 384)
-    sigma_panel = jnp.where(active, applied, jnp.zeros_like(applied))[None]
-    return (sigma_panel, marginal)
+    )(quad_weight, live_block_rows[:, 0], panel[0], jnp.transpose(inv_diag[0], (1, 0, 2)), sigma_rows[0])
+    return (sigma_panel[None], marginal)
 
 
 def solution(mesh):

time: 97.6 us -> 93.8 us (0.961)
  local copies, waits for them, and re-layouts: 6.88 us -> 4.1 us
    reshape x1 -> x0, local copies, waits for them, and re-layouts: 1.18 us -> none  [on_device(): negated.reshape(3, 2, T, T)]
    unnamed x8 -> x2, local copies, waits for them, and re-layouts: 3.67 us -> 4.1 us
where the time goes in v3:
time: 93.8 us; the launch traced here: 93.6 us
  Pallas kernels  88.2 us (94%)
  local copies, waits for them, and re-layouts  4.1 us (4%)
  between operations  1.29 us (1%)
    pallas_call x1, Pallas kernels, on_device(): pl.pallas_call(kernel, out_shape=(jax.ShapeDtypeStruct((T, 2, 384), bf16)...  88.2 us
    unnamed x2, local copies, waits for them, and re-layouts  4.1 us

profile of v3, /device:TPU:1, one launch (start us, length us, event | category | flops | bytes accessed | tf_op | source)
XLA Modules:
  0.0 93.6 jit_solution(7753005340221748006)
XLA Ops:
  1.3 88.2 %shard_map.68 = (bf16[128,2,384]{2,1,0:T(2,128)(2,1)}, f32[2,384,384]{2,1,0:T(8,128)}) custom-call(f32[1]{0:T(128)S(6)} %copy.9.w, s32[2]{0:T(128)} %bitcast.11, bf16[128,2,384]{2,1,0:T(2,128)(2,1)} %bitcast.9, bf16[6,2,384]{2,1,0:T(2,128)(2,1)} %bitcast.10, bf16[512,2048]{1,0:T(8,128)(2,1)} %bitcast.7), custom_call_target="tpu_custom_call" | custom-call | tf_op jit(solution)/shard_map/pallas_call | solution.py:283
  89.5 1.7 %copy.10 = bf16[1,128,2,384]{3,2,1,0:T(2,128)(2,1)} copy(bf16[1,128,2,384]{3,2,1,0:T(2,128)(2,1)} %bitcast.8) | data formatting | bytes 393216
  91.2 2.4 %copy.11 = f32[2,384,384]{2,1,0:T(8,128)} copy(f32[2,384,384]{2,1,0:T(8,128)} %get-tuple-element.9) | data formatting | bytes 2359296

commit v4 on v3

--- a/solution.py
+++ b/solution.py
@@ -40,8 +40,8 @@
 
 
 def kernel(
-    w, live, panel, inv, sig, out, marg,
-    m, iv, ob, sg, q, f, wp, pr, sb, zb, ma,
+    w, live_far, panel_far, inv_far, sig, out, marg,
+    live, panel, inv, lsem, m, iv, ob, sg, q, f, wp, pr, sb, zb, ma,
     d0, d1, d2, dr0, dr1, dr2, e0, e1, e2, yr0, yr1, yr2, xs0, xs1, xs2, zs0, zs1, zs2, g0, g1, g2,
     ssig, s1, r1, s2, r2, s3, r3, s4, r4, s5, r5, s6, r6, sm, rm,
     sd, rd, sy, ry, sx, rx, sz, rz, sg2, rg2, sc, rc,
@@ -58,6 +58,12 @@
     right, left = (x + 1) % NX, (x + 3) % NX
     partner, opposite = place(y, x, z, 1 - k), place(y, x, (z + 4) % NZ, k)
 
+    near = [
+        pltpu.make_async_copy(a, b, lsem.at[n])
+        for n, (a, b) in enumerate(((live_far, live), (panel_far, panel), (inv_far, inv)))
+    ]
+    for copy in near:
+        copy.start()
     barrier = pltpu.get_barrier_semaphore()
     greet = [partner]
     greet += [place(y, (x + a) % NX, z, c) for a in range(1, NX) for c in range(2)]
@@ -68,6 +74,8 @@
     sigma_copy = pltpu.make_async_copy(sig, sg, ssig)
     sigma_copy.start()
     weight = w[0]
+    for copy in near:
+        copy.wait()
     rows = lax.broadcasted_iota(jnp.int32, (T, T), 0)
     active = [rows < live[s] for s in range(2)]
     for j in range(3):
@@ -279,6 +287,7 @@
     dma = pltpu.SemaphoreType.DMA
     vmem = pl.BlockSpec(memory_space=pltpu.VMEM)
     smem = pl.BlockSpec(memory_space=pltpu.SMEM)
+    hbm = pl.BlockSpec(memory_space=pltpu.HBM)
     rows = [(j + 1) * T for j in range(3)]
     sigma_panel, marginal = pl.pallas_call(
         kernel,
@@ -286,9 +295,13 @@
             jax.ShapeDtypeStruct((T, 2, 384), bf16),
             jax.ShapeDtypeStruct((2, 384, 384), f32),
         ),
-        in_specs=[smem, smem, vmem, vmem, pl.BlockSpec(memory_space=pl.ANY)],
+        in_specs=[smem, hbm, hbm, hbm, hbm],
         out_specs=(vmem, vmem),
         scratch_shapes=[
+            pltpu.SMEM((2,), jnp.int32),
+            pltpu.VMEM((T, 2, 384), bf16),
+            pltpu.VMEM((6, 2, 384), bf16),
+            dma((3,)),
             pltpu.VMEM((CHUNKS, T, T), bf16),
             pltpu.VMEM((2, 8, 384), f32),
             pltpu.VMEM((3, T, T), f32),
@@ -325,9 +338,15 @@
             dma((3,)), dma((3,)),
         ],
         compiler_params=pltpu.CompilerParams(
-            collective_id=0, has_side_effects=True, vmem_limit_bytes=56 * 1024 * 1024
+            collective_id=0, has_side_effects=True, vmem_limit_bytes=24 * 1024 * 1024
         ),
-    )(quad_weight, live_block_rows[:, 0], panel[0], jnp.transpose(inv_diag[0], (1, 0, 2)), sigma_rows[0])
+    )(
+        quad_weight,
+        *(
+            pltpu.with_memory_space_constraint(v, pltpu.HBM)
+            for v in (live_block_rows[:, 0], panel[0], jnp.transpose(inv_diag[0], (1, 0, 2)), sigma_rows[0])
+        ),
+    )
     return (sigma_panel[None], marginal)
 
 

time: 93.8 us -> 89.8 us (0.957)
  local copies, waits for them, and re-layouts: 4.1 us -> 1.69 us
  Pallas kernels: 88.2 us -> 86.7 us
    unnamed x2, local copies, waits for them, and re-layouts: 4.1 us -> 1.69 us
    pallas_call x1, Pallas kernels: 88.2 us -> 86.7 us  [on_device(): pl.pallas_call(kernel, out_shape=(jax.ShapeDtypeStruct((T, 2, 384), bf16)...]
where the time goes in v4:
time: 89.8 us; the launch traced here: 89.6 us
  Pallas kernels  86.7 us (97%)
  local copies, waits for them, and re-layouts  1.69 us (2%)
  between operations  1.29 us (1%)
    pallas_call x1, Pallas kernels, on_device(): pl.pallas_call(kernel, out_shape=(jax.ShapeDtypeStruct((T, 2, 384), bf16)...  86.7 us

profile of v4, /device:TPU:1, one launch (start us, length us, event | category | flops | bytes accessed | tf_op | source)
XLA Modules:
  0.0 89.6 jit_solution(8516928903055376698)
XLA Ops:
  1.3 86.7 %shard_map.68 = (bf16[128,2,384]{2,1,0:T(2,128)(2,1)S(1)}, f32[2,384,384]{2,1,0:T(8,128)S(1)}) custom-call(f32[1]{0:T(128)S(6)} %copy.9.w, s32[2]{0:T(128)} %bitcast.11, bf16[128,2,384]{2,1,0:T(2,128)(2,1)} %bitcast.9, bf16[6,2,384]{2,1,0:T(2,128)(2,1)} %bitcast.10, bf16[512,2048]{1,0:T(8,128)(2,1)} %bitcast.8), custom_call_target="tpu_custom_call" | custom-call | tf_op jit(solution)/shard_map/pallas_call | solution.py:292
  87.9 0.7 copy.10
  88.6 1.0 %copy.11 = f32[2,384,384]{2,1,0:T(8,128)} copy(f32[2,384,384]{2,1,0:T(8,128)S(1)} %get-tuple-element.9) | data formatting | bytes 2359296
